TPU v7x, 256 devices: a whole 4x4x8 slice. The times are simulated.
256 devices in a mesh: chan: 8 (over z), seqo: 4 (over y), seqi: 8 (over x, core).
Axes of the slice: x: 4, y: 4, z: 8, core: 2. Of those that a mesh axis runs over, the one named last changes fastest.
Arguments:
- gate_in: bfloat16 [65536, 4096], P(('seqo', 'seqi'), 'chan'), may hold values from -6 to 6
- value_in: bfloat16 [65536, 4096], P(('seqo', 'seqi'), 'chan'), may hold values from -6 to 6
- out_gate: bfloat16 [65536, 4096], P(('seqo', 'seqi'), 'chan'), may hold values from -6 to 6
- residual: bfloat16 [65536, 4096], P(('seqo', 'seqi'), 'chan'), may hold values from -200 to 200
- filters: bfloat16 [8, 32, 6, 65536], P('chan', ('seqo', 'seqi')), may hold values from -5 to 5
- kept_index: int32 [8, 128], P('chan'), may hold values from -1 to 511, as said below
- kept_owner: int32 [8, 128], P('chan'), may hold values from -1 to 31, as said below
- skip_bias: float32 [4096], P('chan'), may hold values from -1 to 1
- norm_gain: float32 [4096], P('chan'), may hold values from 0.5 to 1.5
Outputs:
- hidden_out: bfloat16 [65536, 4096], P(('seqo', 'seqi'), 'chan')
- normed: bfloat16 [65536, 4096], P(('seqo', 'seqi'), 'chan')
Inputs may be any that keep to these rules, and one draw needn't show every extreme that they name: `kept_index`: row s lists the kept channels of slab s in rising order, distinct, between 64 and 128 of them, followed by -1 in the unused slots; some slab lists exactly 128. `kept_owner`: -1 exactly where kept_index is -1, else a device index along seqo+seqi. Within a slab no device owns more than 6 kept channels, and in every slab some device owns exactly 6.
All inputs are finite; a program needn't handle non-finite values.
Results may differ from a plain program's by a relative error of at most 0.005.
Values may be sent and summed in bfloat16 or wider, within the bound.
A program may use at most 128 MiB of HBM per device.

v0:
```python
import jax
import jax.numpy as jnp
from jax import lax
from jax.sharding import PartitionSpec as P

FA = 512


norm_eps = 1e-06
highest = lax.Precision.HIGHEST


def owner_ranks(owners_row):
    is_live = owners_row >= 0
    slot_count = owners_row.shape[0]
    token_position = jnp.arange(slot_count, dtype=jnp.int32)
    earlier = (
        (owners_row[:, None] == owners_row[None, :])
        & is_live[None, :]
        & (token_position[None, :] < token_position[:, None])
    )
    return jnp.sum(earlier.astype(jnp.int32), axis=1)


def angle_table(first, second, modulus):
    product = first[:, None] * second[None, :] % modulus
    return 2.0 * jnp.pi / modulus * product.astype(jnp.float32)


def causal_convolve(signals, kernels, outer_len):
    channels, length = signals.shape
    inner_len = 2 * length // outer_len
    total_len = outer_len * inner_len
    outer_steps = jnp.arange(outer_len, dtype=jnp.int32)
    half_steps = jnp.arange(outer_len // 2, dtype=jnp.int32)
    inner_steps = jnp.arange(inner_len, dtype=jnp.int32)
    outer_angle = angle_table(outer_steps, half_steps, outer_len)
    twist_angle = angle_table(outer_steps, inner_steps, total_len)
    inner_angle = angle_table(inner_steps, inner_steps, inner_len)
    outer_cos = jnp.cos(outer_angle)
    outer_sin = jnp.sin(outer_angle)
    twist_cos = jnp.cos(twist_angle)
    twist_sin = jnp.sin(twist_angle)
    inner_cos = jnp.cos(inner_angle)
    inner_sin = jnp.sin(inner_angle)
    outer_fwd = jnp.concatenate([outer_cos, -outer_sin], axis=0)
    inner_fwd = jnp.concatenate(
        [
            jnp.concatenate([inner_cos, -inner_sin], axis=1),
            jnp.concatenate([inner_sin, inner_cos], axis=1),
        ],
        axis=0,
    )
    inner_back = jnp.concatenate(
        [
            jnp.concatenate([inner_cos, inner_sin], axis=1),
            jnp.concatenate([-inner_sin, inner_cos], axis=1),
        ],
        axis=0,
    )
    outer_back = jnp.concatenate([outer_cos, -outer_sin], axis=0)

    def forward(series):
        blocks = series.astype(jnp.float32).reshape(channels, outer_len // 2, inner_len)
        first = jnp.einsum("ka,cab->ckb", outer_fwd, blocks, precision=highest)
        first_re = first[:, :outer_len]
        first_im = first[:, outer_len:]
        turned_re = first_re * twist_cos + first_im * twist_sin
        turned_im = first_im * twist_cos - first_re * twist_sin
        stacked = jnp.concatenate([turned_re, turned_im], axis=2)
        spec = jnp.einsum("ckb,bj->ckj", stacked, inner_fwd, precision=highest)
        return (spec[:, :, :inner_len], spec[:, :, inner_len:])

    signal_re, signal_im = forward(signals)
    kernel_re, kernel_im = forward(kernels)
    joint_re = signal_re * kernel_re - signal_im * kernel_im
    joint_im = signal_re * kernel_im + signal_im * kernel_re
    joint = jnp.concatenate([joint_re, joint_im], axis=2)
    back = jnp.einsum("ckj,jb->ckb", joint, inner_back, precision=highest)
    back_re = back[:, :, :inner_len]
    back_im = back[:, :, inner_len:]
    untwist_re = back_re * twist_cos - back_im * twist_sin
    untwist_im = back_im * twist_cos + back_re * twist_sin
    untwisted = jnp.concatenate([untwist_re, untwist_im], axis=1)
    result = jnp.einsum("ka,ckb->cab", outer_back, untwisted, precision=highest)
    return (result / total_len).reshape(channels, length)


def local(
    gate_in, value_in, out_gate, residual, filters, kept_index, kept_owner, skip_bias, norm_gain
):
    tok_rows, slab_width = gate_in.shape
    own_slots = filters.shape[2]
    length = filters.shape[3]
    outer_devices = lax.axis_size("seqo")
    inner_devices = lax.axis_size("seqi")
    owner_count = outer_devices * inner_devices
    gated_prod = (gate_in.astype(jnp.float32) * value_in.astype(jnp.float32)).astype(jnp.bfloat16)
    index_row = kept_index[0]
    owners_row = kept_owner[0]
    is_live = owners_row >= 0
    slot_ranks = owner_ranks(owners_row)
    target = jnp.where(is_live, slot_ranks * owner_count + owners_row, -1)
    buffer_rows = jnp.arange(own_slots * owner_count, dtype=jnp.int32)
    select = (buffer_rows[:, None] == target[None, :]).astype(jnp.bfloat16)
    channel_pos = jnp.arange(slab_width, dtype=jnp.int32)
    spread = ((index_row[:, None] == channel_pos[None, :]) & is_live[:, None]).astype(jnp.bfloat16)
    picker = jnp.dot(select, spread, preferred_element_type=jnp.float32).astype(jnp.bfloat16)
    outgoing = lax.dot_general(
        picker, gated_prod, (((1,), (1,)), ((), ())), preferred_element_type=jnp.float32
    ).astype(jnp.bfloat16)
    incoming = lax.all_to_all(
        outgoing.reshape(own_slots, owner_count, tok_rows),
        ("seqo", "seqi"),
        split_axis=1,
        concat_axis=1,
        tiled=True,
    )
    convolved = causal_convolve(incoming.reshape(own_slots, length), filters[0, 0], FA)
    returned = lax.all_to_all(
        convolved.reshape(own_slots, owner_count, tok_rows),
        ("seqo", "seqi"),
        split_axis=1,
        concat_axis=1,
        tiled=True,
    )
    returned = returned.reshape(own_slots * owner_count, tok_rows)
    safe_target = jnp.where(is_live, target, 0)
    kept_rows = jnp.take(returned, safe_target, axis=0)
    put_at = jnp.where(is_live, index_row, slab_width)
    conv_cols = (
        jnp.zeros((tok_rows, slab_width), jnp.float32).at[:, put_at].set(kept_rows.T, mode="drop")
    )
    gated_wide = gated_prod.astype(jnp.float32)
    mixed_out = out_gate.astype(jnp.float32) * (conv_cols + skip_bias[None, :] * gated_wide)
    hidden_out = (residual.astype(jnp.float32) + mixed_out).astype(jnp.bfloat16)
    hidden_wide = hidden_out.astype(jnp.float32)
    squares = jnp.sum(hidden_wide * hidden_wide, axis=1)
    row_total = lax.psum(squares, "chan")
    width_all = slab_width * lax.axis_size("chan")
    scaling = lax.rsqrt(row_total / width_all + norm_eps)
    normed = (hidden_wide * scaling[:, None] * norm_gain[None, :]).astype(jnp.bfloat16)
    return (hidden_out, normed)


def solution(mesh):
    in_specs = (
        P(("seqo", "seqi"), "chan"),
        P(("seqo", "seqi"), "chan"),
        P(("seqo", "seqi"), "chan"),
        P(("seqo", "seqi"), "chan"),
        P("chan", ("seqo", "seqi"), None, None),
        P("chan", None),
        P("chan", None),
        P("chan"),
        P("chan"),
    )
    out_specs = (P(("seqo", "seqi"), "chan"), P(("seqo", "seqi"), "chan"))
    return jax.shard_map(local, mesh=mesh, in_specs=in_specs, out_specs=out_specs, check_vma=False)
```

profile of v0, /device:TPU:0, one launch (start us, length us, event | category | flops | bytes accessed | tf_op | source)
XLA Modules:
  0.0 186.3 jit_solution(6840904414468012201)
XLA Ops:
  3.5 2.9 %copy.66 = bf16[2048,512]{0,1:T(8,128)(2,1)S(1)} copy(bf16[2048,512]{1,0:T(8,128)(2,1)} %param.9) | data formatting | bytes 4194304 | tf_op args[0]
  6.5 4.6 %copy.67 = bf16[2048,512]{0,1:T(8,128)(2,1)} copy(bf16[2048,512]{1,0:T(8,128)(2,1)} %param.10) | data formatting | bytes 4194304 | tf_op args[1]
  11.1 2.5 %convolution_convert_fusion = bf16[192,2048]{1,0:T(8,128)(2,1)S(1)} fusion(bf16[2048,512]{0,1:T(8,128)(2,1)} %copy.67, bf16[2048,512]{0,1:T(8,128)(2,1)S(1)} %copy.66, s32[128]{0:T(128)S(1)} %bitcast.65, pred[128]{0:T(512)(128)(4,1)S(1)} %get-tuple-element.24, s32[128]{0:T(128)S(1)} %fusion.70), kind=kOutput, calls=%fused_computation.35 | convolution fusion | flops 432660480 | bytes 4981888 | tf_op jit(solution)/shard_map/dot_general | solution.py:109
  15.0 6.2 %all-to-all-start = ((bf16[6,32,2048]{2,0,1:T(8,128)(2,1)}), bf16[6,32,2048]{2,0,1:T(8,128)(2,1)}, u32[]{:S(2)}, u32[]{:S(2)}) async-start(bf16[6,32,2048]{2,0,1:T(8,128)(2,1)} %copy.68), calls=%async_computation | async-start | bytes 2097152 | tf_op jit(solution)/shard_map/all_to_all | solution.py:112
  29.8 2.1 %sine_negate_fusion = (f32[512,256]{1,0:T(8,128)S(1)}, f32[512,256]{1,0:T(8,128)S(1)}) fusion(), kind=kLoop, calls=%fused_computation.64 | loop fusion | flops 1966080 | bytes 1048576 | tf_op jit(solution)/shard_map/neg | solution.py:46
  31.9 4.6 %convolution_bitcast_fusion = f32[6,1024,256]{1,2,0:T(8,128)} fusion(bf16[1,6,256,256]{3,1,2,0:T(8,128)(2,1)S(1)} %bitcast.63, f32[512,256]{1,0:T(8,128)S(1)} %get-tuple-element.26, f32[512,256]{1,0:T(8,128)S(1)} %get-tuple-element.27), kind=kOutput, calls=%fused_computation.33 | convolution fusion | flops 4832100352 | bytes 8126464 | tf_op jit(solution)/shard_map/ka,cab->ckb/dot_general | solution.py:65
  38.4 2.7 %copy.69 = bf16[6,32,2048]{2,1,0:T(8,128)(2,1)} copy(bf16[6,32,2048]{2,0,1:T(8,128)(2,1)} %all-to-all-done) | data formatting | bytes 1572864 | tf_op jit(solution)/shard_map/all_to_all | solution.py:112
  41.0 2.8 %reshape.146 = bf16[6,256,256]{2,1,0:T(8,128)(2,1)} reshape(bf16[6,32,2048]{2,1,0:T(8,128)(2,1)} %copy.69) | data formatting | bytes 1572864 | tf_op jit(solution)/shard_map/reshape | solution.py:64
  43.9 4.8 %convolution_bitcast_fusion.1 = f32[6,1024,256]{1,2,0:T(8,128)S(1)} fusion(bf16[6,256,256]{2,1,0:T(8,128)(2,1)} %reshape.146, f32[512,256]{1,0:T(8,128)S(1)} %get-tuple-element.26, f32[512,256]{1,0:T(8,128)S(1)} %get-tuple-element.27), kind=kOutput, calls=%fused_computation.34 | convolution fusion | flops 4832100352 | bytes 8126464 | tf_op jit(solution)/shard_map/ka,cab->ckb/dot_general | solution.py:65
  48.8 2.9 %multiply_add_fusion.3 = (f32[6,512,256]{1,2,0:T(8,128)S(1)}, f32[6,512,256]{1,2,0:T(8,128)S(1)}, f32[6,512,256]{1,2,0:T(8,128)S(1)}, f32[6,512,256]{1,2,0:T(8,128)}) fusion(f32[6,1024,256]{1,2,0:T(8,128)S(1)} %convolution_bitcast_fusion.1, f32[512,256]{0,1:T(8,128)S(1)} %copy-done.8, f32[512,256]{0,1:T(8,128)S(1)} %copy-done.6, f32[6,1024,256]{1,2,0:T(8,128)S(1)} %bitcast.60), kind=kLoop, calls=%fused_computation.32 | loop fusion | flops 9437184 | bytes 26214400 | tf_op jit(solution)/shard_map/add | solution.py:68
  51.7 12.5 %fusion = f32[6,512,512]{1,2,0:T(8,128)S(1)} fusion(f32[6,512,256]{1,2,0:T(8,128)S(1)} %get-tuple-element.17, f32[6,512,256]{1,2,0:T(8,128)S(1)} %get-tuple-element.16, f32[256,256]{0,1:T(8,128)S(1)} %copy-done.12, f32[256,256]{0,1:T(8,128)S(1)} %copy-done.11, f32[256,256]{0,1:T(8,128)S(1)} %fusion.66), kind=kOutput, calls=%fused_computation.2 | convolution fusion | flops 9666035712 | bytes 13369344 | tf_op jit(solution)/shard_map/ckb,bj->ckj/dot_general | solution.py:71
  64.2 12.8 %fusion.4 = f32[6,512,512]{1,2,0:T(8,128)S(1)} fusion(f32[6,512,256]{1,2,0:T(8,128)S(1)} %get-tuple-element.20, f32[6,512,256]{1,2,0:T(8,128)S(1)} %copy-done.3, f32[256,256]{0,1:T(8,128)S(1)} %copy-done.12, f32[256,256]{0,1:T(8,128)S(1)} %copy-done.11, f32[256,256]{0,1:T(8,128)S(1)} %fusion.66), kind=kOutput, calls=%fused_computation.6 | convolution fusion | flops 9666035712 | bytes 13369344 | tf_op jit(solution)/shard_map/ckb,bj->ckj/dot_general | solution.py:71
  78.6 14.0 %fusion.8 = f32[6,512,512]{1,2,0:T(8,128)S(1)} fusion(f32[6,512,256]{1,2,0:T(8,128)S(1)} %get-tuple-element.13, f32[6,512,256]{1,2,0:T(8,128)S(1)} %get-tuple-element.12, f32[256,256]{0,1:T(8,128)} %get-tuple-element.29, f32[256,256]{0,1:T(8,128)} %copy-done.10, f32[256,256]{0,1:T(8,128)} %get-tuple-element.28), kind=kOutput, calls=%fused_computation.10 | convolution fusion | flops 9666035712 | bytes 13369344 | tf_op jit(solution)/shard_map/ckj,jb->ckb/dot_general | solution.py:79
  93.7 6.7 %multiply_bitcast_fusion = f32[6,256,256]{1,2,0:T(8,128)} fusion(f32[6,512,256]{1,2,0:T(8,128)S(1)} %get-tuple-element.15, f32[6,512,256]{1,2,0:T(8,128)S(1)} %get-tuple-element.14, f32[512,256]{1,0:T(8,128)S(1)} %get-tuple-element.26, f32[512,256]{1,0:T(8,128)S(1)} %copy-done.5), kind=kOutput, calls=%fused_computation.38 | convolution fusion | flops 4834066432 | bytes 8912896 | tf_op jit(solution)/shard_map/ka,ckb->cab/dot_general | solution.py:85
  102.5 2.3 %copy.81 = f32[6,32,2048]{2,0,1:T(8,128)} copy(f32[6,32,2048]{2,1,0:T(8,128)S(1)} %reshape_reshape.3) | data formatting | bytes 3145728 | tf_op jit(solution)/shard_map/reshape;reshape | solution.py:121
  104.8 5.6 %all-to-all-start.1 = ((f32[6,32,2048]{2,0,1:T(8,128)}), f32[6,32,2048]{2,0,1:T(8,128)S(1)}, u32[]{:S(2)}, u32[]{:S(2)}) async-start(f32[6,32,2048]{2,0,1:T(8,128)} %copy.81), calls=%async_computation.1 | async-start | bytes 4194304 | tf_op jit(solution)/shard_map/all_to_all | solution.py:120
  110.4 4.0 %copy.64 = bf16[2048,512]{0,1:T(8,128)(2,1)} copy(bf16[2048,512]{1,0:T(8,128)(2,1)} %param.12) | data formatting | bytes 4194304 | tf_op args[3]
  114.4 4.0 %copy.65 = bf16[2048,512]{0,1:T(8,128)(2,1)} copy(bf16[2048,512]{1,0:T(8,128)(2,1)} %param.11) | data formatting | bytes 4194304 | tf_op args[2]
  118.4 22.1 %all-to-all-done.1 = f32[6,32,2048]{2,0,1:T(8,128)S(1)} async-done(((f32[6,32,2048]{2,0,1:T(8,128)}), f32[6,32,2048]{2,0,1:T(8,128)S(1)}, u32[]{:S(2)}, u32[]{:S(2)}) %all-to-all-start.1) | async-done | bytes 1572896 | tf_op jit(solution)/shard_map/all_to_all | solution.py:120
  142.6 6.8 %scatter_custom_fusion = f32[2048,512]{0,1:T(8,128)} fusion(s32[128]{0:T(128)S(1)} %get-tuple-element.23, f32[]{:T(128)} %constant.60.clone.1, f32[]{:T(128)} %constant.76.clone.1, pred[128]{0:T(512)(128)(4,1)S(1)} %get-tuple-element.25, f32[192,2048]{1,0:T(8,128)} %bitcast.61, s32[1024]{0:T(1024)S(1)} %pad_clamp_fusion), kind=kCustom, calls=%fused_computation.36 | custom fusion | flops 262144 | bytes 5771784 | tf_op jit(solution)/shard_map/scatter | solution.py:132
  149.4 7.6 %fusion.16 = (f32[2048]{0:T(1024)S(1)}, bf16[2048,512]{0,1:T(8,128)(2,1)}) fusion(f32[2048,512]{0,1:T(8,128)} %scatter_custom_fusion, bf16[2048,512]{0,1:T(8,128)(2,1)} %copy.67, bf16[2048,512]{0,1:T(8,128)(2,1)S(1)} %copy-done.1, f32[512]{0:T(512)S(1)} %copy-done.15, bf16[2048,512]{0,1:T(8,128)(2,1)} %copy.65, bf16[2048,512]{0,1:T(8,128)(2,1)} %copy.64), kind=kLoop, calls=%fused_computation.20 | loop fusion | flops 15726592 | bytes 14690304 | tf_op jit(solution)/shard_map/reduce_sum | solution.py:138
  157.1 19.3 %psum.7 = f32[2048]{0:T(1024)S(1)} all-reduce(f32[2048]{0:T(1024)S(1)} %get-tuple-element.10), channel_id=1, replica_groups=mesh['chan'=8,'seqo'=4,'seqi'=8] {'chan'}, use_global_device_ids=true, to_apply=%region_3.4 | all-reduce | flops 2048 | bytes 16384 | tf_op jit(solution)/shard_map/psum | solution.py:139
  176.4 3.9 %copy.83 = bf16[2048,512]{1,0:T(8,128)(2,1)} copy(bf16[2048,512]{0,1:T(8,128)(2,1)} %get-tuple-element.11) | data formatting | bytes 4194304
  182.2 3.9 %copy.84 = bf16[2048,512]{1,0:T(8,128)(2,1)} copy(bf16[2048,512]{0,1:T(8,128)(2,1)} %fusion.18) | data formatting | bytes 4194304
  (62 shorter events, 23.5 us)
Async XLA Ops:
  6.5 7.1 %copy-start = (bf16[2048,512]{0,1:T(8,128)(2,1)}, bf16[2048,512]{0,1:T(8,128)(2,1)S(1)}, u32[]{:S(2)}) copy-start(bf16[2048,512]{0,1:T(8,128)(2,1)S(1)} %copy.66) | copy-start | bytes 6291460
  6.5 4.6 %copy-start.17 = (s32[1,128]{1,0:T(1,128)S(1)}, s32[1,128]{1,0:T(1,128)}, u32[]{:S(2)}) copy-start(s32[1,128]{1,0:T(1,128)} %param.14) | copy-start | bytes 1540
  15.0 16.9 %copy-start.13 = (bf16[1,1,6,65536]{3,2,1,0:T(8,128)(2,1)S(1)}, bf16[1,1,6,65536]{3,2,1,0:T(8,128)(2,1)}, u32[]{:S(2)}) copy-start(bf16[1,1,6,65536]{3,2,1,0:T(8,128)(2,1)} %param.13) | copy-start | bytes 2359300
  15.0 23.4 %all-to-all-start = ((bf16[6,32,2048]{2,0,1:T(8,128)(2,1)}), bf16[6,32,2048]{2,0,1:T(8,128)(2,1)}, u32[]{:S(2)}, u32[]{:S(2)}) async-start(bf16[6,32,2048]{2,0,1:T(8,128)(2,1)} %copy.68), calls=%async_computation | async-start | bytes 2097152 | tf_op jit(solution)/shard_map/all_to_all | solution.py:112
  28.0 36.2 %copy-start.10 = (f32[256,256]{0,1:T(8,128)}, f32[256,256]{0,1:T(8,128)S(1)}, u32[]{:S(2)}) copy-start(f32[256,256]{0,1:T(8,128)S(1)} %fusion.66) | copy-start | bytes 786436
  31.8 12.0 %copy-start.4 = (f32[512,256]{1,0:T(8,128)}, f32[512,256]{1,0:T(8,128)S(1)}, u32[]{:S(2)}) copy-start(f32[512,256]{1,0:T(8,128)S(1)} %get-tuple-element.27) | copy-start | bytes 1572868
  38.3 10.4 %slice-start = ((s8[6291456]{0:T(1024)(128)(4,1)}), s8[2097152]{0:T(1024)(128)(4,1)S(1)}, s32[]{:S(2)}) async-start(s8[6291456]{0:T(1024)(128)(4,1)} %bitcast.59), calls=%async_computation.2 | async-start | bytes 4194304
  43.9 4.9 %slice-start.1 = ((s8[6291456]{0:T(1024)(128)(4,1)}), s8[4194304]{0:T(1024)(128)(4,1)S(1)}, s32[]{:S(2)}) async-start(s8[6291456]{0:T(1024)(128)(4,1)} %bitcast.59), calls=%async_computation.3 | async-start | bytes 8388608
  43.9 4.9 %copy-start.6 = (f32[512,256]{0,1:T(8,128)S(1)}, f32[512,256]{0,1:T(8,128)}, u32[]{:S(2)}) copy-start(f32[512,256]{0,1:T(8,128)} %copy.71) | copy-start | bytes 1572868
  43.9 4.9 %copy-start.8 = (f32[512,256]{0,1:T(8,128)S(1)}, f32[512,256]{0,1:T(8,128)}, u32[]{:S(2)}) copy-start(f32[512,256]{0,1:T(8,128)} %copy.72) | copy-start | bytes 1572868
  48.8 2.9 %copy-start.11 = (f32[256,256]{0,1:T(8,128)S(1)}, f32[256,256]{0,1:T(8,128)}, u32[]{:S(2)}) copy-start(f32[256,256]{0,1:T(8,128)} %get-tuple-element.28) | copy-start | bytes 786436
  48.8 2.9 %copy-start.12 = (f32[256,256]{0,1:T(8,128)S(1)}, f32[256,256]{0,1:T(8,128)}, u32[]{:S(2)}) copy-start(f32[256,256]{0,1:T(8,128)} %get-tuple-element.29) | copy-start | bytes 786436
  51.7 12.5 %copy-start.3 = (f32[6,512,256]{1,2,0:T(8,128)S(1)}, f32[6,512,256]{1,2,0:T(8,128)}, u32[]{:S(2)}) copy-start(f32[6,512,256]{1,2,0:T(8,128)} %get-tuple-element.21) | copy-start | bytes 9437188
  78.6 14.0 %copy-start.7 = (f32[512,256]{0,1:T(8,128)S(1)}, f32[512,256]{0,1:T(8,128)}, u32[]{:S(2)}) copy-start(f32[512,256]{0,1:T(8,128)} %copy.71) | copy-start | bytes 1572868
  78.6 14.0 %copy-start.9 = (f32[512,256]{0,1:T(8,128)S(1)}, f32[512,256]{0,1:T(8,128)}, u32[]{:S(2)}) copy-start(f32[512,256]{0,1:T(8,128)} %copy.72) | copy-start | bytes 1572868
  92.6 1.0 copy-start.5
  104.8 35.7 %all-to-all-start.1 = ((f32[6,32,2048]{2,0,1:T(8,128)}), f32[6,32,2048]{2,0,1:T(8,128)S(1)}, u32[]{:S(2)}, u32[]{:S(2)}) async-start(f32[6,32,2048]{2,0,1:T(8,128)} %copy.81), calls=%async_computation.1 | async-start | bytes 4194304 | tf_op jit(solution)/shard_map/all_to_all | solution.py:120
  114.4 4.0 %copy-start.14 = (s32[1,128]{1,0:T(1,128)S(1)}, s32[1,128]{1,0:T(1,128)}, u32[]{:S(2)}) copy-start(s32[1,128]{1,0:T(1,128)} %param.15) | copy-start | bytes 1540
  142.6 6.9 %copy-start.1 = (bf16[2048,512]{0,1:T(8,128)(2,1)S(1)}, bf16[2048,512]{0,1:T(8,128)(2,1)}, u32[]{:S(2)}) copy-start(bf16[2048,512]{0,1:T(8,128)(2,1)} %copy-done) | copy-start | bytes 6291460
  142.6 6.9 %copy-start.15 = (f32[512]{0:T(512)S(1)}, f32[512]{0:T(512)}, u32[]{:S(2)}) copy-start(f32[512]{0:T(512)} %param.16) | copy-start | bytes 6148
  157.1 23.2 %copy-start.2 = (bf16[2048,512]{0,1:T(8,128)(2,1)S(1)}, bf16[2048,512]{0,1:T(8,128)(2,1)}, u32[]{:S(2)}) copy-start(bf16[2048,512]{0,1:T(8,128)(2,1)} %get-tuple-element.11) | copy-start | bytes 6291460
  157.1 23.2 %copy-start.16 = (f32[512]{0:T(512)S(1)}, f32[512]{0:T(512)}, u32[]{:S(2)}) copy-start(f32[512]{0:T(512)} %param.17) | copy-start | bytes 6148
where the time goes:
time: 190 us; the launch traced here: 186 us
  matrix products  57.9 us (30%)
  local copies, waits for them, and re-layouts  38.8 us (20%)
  other arithmetic  33.4 us (18%)
  waiting for transfers between devices  23.9 us (13%)
  blocking collectives  19.3 us (10%)
  starting transfers between devices  11.8 us (6%)
    dot_general x2, matrix products, forward(): spec = jnp.einsum('ckb,bj->ckj', stacked, inner_fwd, precision=highest)  25.3 us
    unnamed x46, local copies, waits for them, and re-layouts  23.4 us
    all_to_all x1, waiting for transfers between devices, local(): lax.all_to_all(convolved.reshape(own_slots, owner_count, tok_rows), ('seq...  22.1 us
    psum x1, blocking collectives, local(): row_total = lax.psum(squares, 'chan')  19.3 us
    dot_general x1, matrix products, causal_convolve(): back = jnp.einsum('ckj,jb->ckb', joint, inner_back, precision=highest)  14 us
    dot_general x2, matrix products, forward(): first = jnp.einsum('ka,cab->ckb', outer_fwd, blocks, precision=highest)  9.43 us
    reduce_sum x1, other arithmetic, local(): squares = jnp.sum(hidden_wide * hidden_wide, axis=1)  7.64 us
    scatter x1, other arithmetic, local(): jnp.zeros((tok_rows, slab_width), jnp.float32).at[:, put_at]  6.85 us
  transfers between devices with their start and end apart: 2, of which 2 were waited for; matrix products, arithmetic and copies ran while one was open for 12% of the time, Pallas kernels for 0%

commit v1 on v0

v1 whole, which is shorter than its diff:
```python
import functools

import jax
import jax.numpy as jnp
import numpy as np
from jax import lax
from jax.experimental import pallas as pl
from jax.experimental.pallas import tpu as pltpu
from jax.sharding import PartitionSpec as P

norm_eps = 1e-06
LANES = 128
MESH = pl.DeviceIdType.MESH
F32 = jnp.float32
BF16 = jnp.bfloat16


def split_table(table):
    high = table.astype(BF16)
    low = (table - high.astype(np.float64)).astype(BF16)
    return high, low


@functools.lru_cache(maxsize=None)
def tables(rows):
    step = np.arange(rows, dtype=np.float64) + 0.5
    outer = 2.0 * np.pi * np.outer(step, step) / (2 * rows)
    inner_at = np.arange(LANES, dtype=np.float64)
    twist = 2.0 * np.pi * np.outer(step, inner_at - LANES / 2) / (2 * rows * LANES)
    inner = 2.0 * np.pi * np.outer(inner_at, inner_at) / LANES
    outer_tab = np.stack([*split_table(np.cos(outer)), *split_table(-np.sin(outer))])
    twist_tab = np.stack([np.cos(twist), np.sin(twist)]).astype(np.float32)
    cos, sin = np.cos(inner), np.sin(inner)
    forward = np.block([[cos, -sin], [sin, cos]])
    back = np.block([[cos, sin], [-sin, cos]])
    inner_tab = np.stack([*split_table(forward), *split_table(back)])
    return outer_tab, twist_tab, inner_tab


def dot(a, b):
    return jnp.dot(a, b, preferred_element_type=F32)


def iota(shape, dim):
    return lax.broadcasted_iota(jnp.int32, shape, dim)


def main_kernel(
    slots,
    seqo,
    seqi,
    chan,
    index_ref,
    owner_ref,
    skip_ref,
    gate_hbm,
    value_hbm,
    og_hbm,
    res_hbm,
    filt_hbm,
    outer_hbm,
    twist_hbm,
    inner_hbm,
    hid_hbm,
    total_ref,
    gate,
    value,
    og,
    res,
    filt,
    outer,
    twist,
    inner,
    gated,
    base,
    hid,
    wide,
    fwide,
    sent,
    arrived,
    fpair,
    spec,
    turn_re,
    turn_im,
    back,
    ret,
    squares,
    parts,
    load_sem,
    local_sem,
    send_sem,
    recv_sem,
    bsend_sem,
    brecv_sem,
    zsend_sem,
    zrecv_sem,
    out_sem,
):
    owners = seqo * seqi
    pairs = slots // 2
    tok, width = gated.shape
    per = tok // LANES
    rows = per * owners
    live_slots = slots * owners
    me = lax.axis_index("seqo") * seqi + lax.axis_index("seqi")
    mez = lax.axis_index("chan")
    chunks = 4
    crow = tok // chunks
    tile = 256

    def load(src, dst, k):
        return pltpu.make_async_copy(src, dst, load_sem.at[k])

    def gate_loads(c):
        at = pl.ds(c * crow, crow)
        return (
            load(gate_hbm.at[at], gate.at[at], 2 * c),
            load(value_hbm.at[at], value.at[at], 2 * c + 1),
        )

    for c in range(chunks):
        for cp in gate_loads(c):
            cp.start()
    nl = 2 * chunks
    filt_load = load(filt_hbm.at[0, 0], filt, nl)
    outer_load = load(outer_hbm, outer, nl + 1)
    twist_load = load(twist_hbm, twist, nl + 2)
    inner_load = load(inner_hbm, inner, nl + 3)
    og_load = load(og_hbm, og, nl + 4)
    res_load = load(res_hbm, res, nl + 5)
    for cp in (filt_load, outer_load, twist_load, inner_load, og_load, res_load):
        cp.start()

    def plane(i):
        o = lax.rem(me + i, owners)
        return o, {"seqo": o // seqi, "seqi": lax.rem(o, seqi)}

    def column(i):
        return {"chan": lax.rem(mez + i, chan)}

    barrier = pltpu.get_barrier_semaphore()

    def greet_plane(i, carry):
        pl.semaphore_signal(barrier, inc=1, device_id=plane(i)[1], device_id_type=MESH)
        return carry

    def greet_column(i, carry):
        pl.semaphore_signal(barrier, inc=1, device_id=column(i), device_id_type=MESH)
        return carry

    lax.fori_loop(1, owners, greet_plane, 0)
    lax.fori_loop(1, chan, greet_column, 0)

    kmax = index_ref.shape[1]
    own_row = jnp.broadcast_to(owner_ref[...].astype(F32), (kmax, kmax))
    idx_row = jnp.broadcast_to(index_ref[...].astype(F32), (kmax, kmax))
    sub = iota((kmax, kmax), 0)
    lane = iota((kmax, kmax), 1)
    eye = sub == lane
    own_col = jnp.sum(jnp.where(eye, own_row, 0.0), axis=1, keepdims=True)
    idx_col = jnp.sum(jnp.where(eye, idx_row, 0.0), axis=1, keepdims=True)
    same = (jnp.broadcast_to(own_col, (kmax, kmax)) == own_row) & (sub < lane)
    rank = jnp.sum(jnp.where(same, 1.0, 0.0), axis=0, keepdims=True)
    own_one = owner_ref[...].astype(F32)
    slot_row = jnp.where(own_one >= 0.0, rank * owners + own_one, -1.0)
    slot_at = iota((live_slots, kmax), 0).astype(F32)
    select = jnp.where(slot_at == jnp.broadcast_to(slot_row, (live_slots, kmax)), 1.0, 0.0)
    chan_at = iota((kmax, width), 1).astype(F32)
    spread = jnp.where(chan_at == jnp.broadcast_to(idx_col, (kmax, width)), 1.0, 0.0)
    picker = dot(select.astype(BF16), spread.astype(BF16)).astype(BF16)

    for c in range(chunks):
        for cp in gate_loads(c):
            cp.wait()
        at = pl.ds(c * crow, crow)
        prod = (gate[at].astype(F32) * value[at].astype(F32)).astype(BF16)
        gated[at] = prod
        picked = lax.dot_general(
            picker, prod, (((1,), (1,)), ((), ())), preferred_element_type=F32
        )
        for q in range(crow // LANES):
            a = c * (crow // LANES) + q
            for r in range(slots):
                wide[r, pl.ds(a, owners, stride=per), :] = picked[
                    r * owners : (r + 1) * owners, q * LANES : (q + 1) * LANES
                ]

    def span(o):
        return pl.ds(pl.multiple_of(o * per, per), per)

    def exchange(p, src, dst, ssem, rsem):
        mine = pltpu.make_async_copy(
            src.at[p, span(me)], dst.at[p, span(me)], local_sem.at[0]
        )
        mine.start()

        def one(i, carry):
            o, dev = plane(i)
            pltpu.make_async_remote_copy(
                src_ref=src.at[p, span(o)],
                dst_ref=dst.at[p, span(me)],
                send_sem=ssem.at[p],
                recv_sem=rsem.at[p],
                device_id=dev,
                device_id_type=MESH,
            ).start()
            return carry

        lax.fori_loop(1, owners, one, 0)
        mine.wait()

    def whole(p, src, dst, ssem, rsem):
        most = pl.ds(0, rows - per)
        return pltpu.make_async_remote_copy(
            src_ref=src.at[p, most],
            dst_ref=dst.at[p, most],
            send_sem=ssem.at[p],
            recv_sem=rsem.at[p],
            device_id=plane(1)[1],
            device_id_type=MESH,
        )

    for p in range(pairs):
        for ch in range(2):
            sent[p, :, ch * LANES : (ch + 1) * LANES] = wide[2 * p + ch].astype(BF16)
        if p == 0:
            pl.semaphore_wait(barrier, owners + chan - 2)
        exchange(p, sent, arrived, send_sem, recv_sem)

    filt_load.wait()

    def unfold(a, carry):
        taps = filt[:, pl.ds(pl.multiple_of(a * LANES, LANES), LANES)].astype(F32)
        fwide[pl.ds(a, slots, stride=rows), :] = taps
        return carry

    lax.fori_loop(0, rows, unfold, 0, unroll=8)
    for r in range(slots):
        fpair[r // 2, :, (r % 2) * LANES : (r % 2 + 1) * LANES] = fwide[
            r * rows : (r + 1) * rows, :
        ].astype(BF16)

    outer_load.wait()
    twist_load.wait()
    inner_load.wait()

    def forward(x, at):
        re = dot(outer[0, at], x) + dot(outer[1, at], x)
        im = dot(outer[2, at], x) + dot(outer[3, at], x)
        tc, ts = twist[0, at], twist[1, at]
        out = []
        for ch in range(2):
            cut = slice(ch * LANES, (ch + 1) * LANES)
            r, m = re[:, cut], im[:, cut]
            z = jnp.concatenate([r * tc + m * ts, m * tc - r * ts], axis=1).astype(BF16)
            out.append(dot(z, inner[0]) + dot(z, inner[1]))
        return out

    scale = 1.0 / (rows * LANES)

    def filter_pair(p, carry):
        def step(k, carry):
            at = pl.ds(pl.multiple_of(k * tile, tile), tile)
            got = forward(fpair[p], at)
            for ch in range(2):
                spec[2 * p + ch, at] = got[ch] * scale
            return carry

        return lax.fori_loop(0, rows // tile, step, carry)

    lax.fori_loop(0, pairs, filter_pair, 0)

    def convolve_pair(p, carry):
        whole(p, sent, arrived, send_sem, recv_sem).wait_recv()

        def step(k, carry):
            at = pl.ds(pl.multiple_of(k * tile, tile), tile)
            got = forward(arrived[p], at)
            tc, ts = twist[0, at], twist[1, at]
            for ch in range(2):
                cut = slice(ch * LANES, (ch + 1) * LANES)
                kern = spec[2 * p + ch, at]
                sr, si = got[ch][:, :LANES], got[ch][:, LANES:]
                kr, ki = kern[:, :LANES], kern[:, LANES:]
                joint = jnp.concatenate([sr * kr - si * ki, sr * ki + si * kr], axis=1)
                joint = joint.astype(BF16)
                u = dot(joint, inner[2]) + dot(joint, inner[3])
                ur, ui = u[:, :LANES], u[:, LANES:]
                turn_re[at, cut] = (ur * tc - ui * ts).astype(BF16)
                turn_im[at, cut] = (ui * tc + ur * ts).astype(BF16)
            return carry

        lax.fori_loop(0, rows // tile, step, 0)

        def step_back(k, carry):
            at = pl.ds(pl.multiple_of(k * tile, tile), tile)
            u, v = turn_re[...], turn_im[...]
            y = (dot(outer[0, at], u) + dot(outer[1, at], u)) + (
                dot(outer[2, at], v) + dot(outer[3, at], v)
            )
            back[p, at] = y.astype(BF16)
            return carry

        lax.fori_loop(0, rows // tile, step_back, 0)
        exchange(p, back, ret, bsend_sem, brecv_sem)
        return carry

    lax.fori_loop(0, pairs, convolve_pair, 0)

    og_load.wait()
    res_load.wait()
    skip = skip_ref[...]

    def base_step(a, carry):
        at = pl.ds(pl.multiple_of(a * LANES, LANES), LANES)
        base[at] = res[at].astype(F32) + og[at].astype(F32) * (skip * gated[at].astype(F32))
        return carry

    lax.fori_loop(0, per, base_step, 0)

    for p in range(pairs):
        whole(p, back, ret, bsend_sem, brecv_sem).wait_recv()
        for ch in range(2):
            wide[2 * p + ch] = ret[p, :, ch * LANES : (ch + 1) * LANES].astype(F32)

    eye_tile = iota((LANES, LANES), 0) == iota((LANES, LANES), 1)

    def final_step(a, carry):
        at = pl.ds(pl.multiple_of(a * LANES, LANES), LANES)
        got = jnp.concatenate(
            [
                wide[r, pl.ds(a, owners, stride=per), :]
                for r in range(slots)
            ],
            axis=0,
        ).astype(BF16)
        conv = lax.dot_general(got, picker, (((0,), (0,)), ((), ())), preferred_element_type=F32)
        out = (base[at] + og[at].astype(F32) * conv).astype(BF16)
        hid[at] = out
        big = out.astype(F32)
        sq = big * big
        part = sq[:, :LANES]
        for j in range(1, width // LANES):
            part = part + sq[:, j * LANES : (j + 1) * LANES]
        row_sum = jnp.sum(part, axis=1, keepdims=True)
        line = jnp.where(eye_tile, jnp.broadcast_to(row_sum, (LANES, LANES)), 0.0)
        squares[pl.ds(a, 1), :] = jnp.sum(line, axis=0, keepdims=True)
        return carry

    lax.fori_loop(0, per, final_step, 0)
    hid_store = pltpu.make_async_copy(hid, hid_hbm, out_sem.at[0])
    hid_store.start()

    def send_sums(i, carry):
        pltpu.make_async_remote_copy(
            src_ref=squares,
            dst_ref=parts.at[i],
            send_sem=zsend_sem.at[i],
            recv_sem=zrecv_sem.at[i],
            device_id=column(i),
            device_id_type=MESH,
        ).start()
        return carry

    lax.fori_loop(1, chan, send_sums, 0)

    def take_sums(i, acc):
        cp = pltpu.make_async_remote_copy(
            src_ref=squares,
            dst_ref=parts.at[i],
            send_sem=zsend_sem.at[i],
            recv_sem=zrecv_sem.at[i],
            device_id=column(i),
            device_id_type=MESH,
        )
        cp.wait()
        return acc + parts[i]

    total_ref[...] = lax.fori_loop(1, chan, take_sums, squares[...])

    for p in range(pairs):
        whole(p, sent, arrived, send_sem, recv_sem).wait_send()
        whole(p, back, ret, bsend_sem, brecv_sem).wait_send()
    hid_store.wait()


def norm_kernel(width_all, hid_ref, total_ref, gain_ref, out_ref, normed_ref):
    groups = hid_ref.shape[0] // LANES
    eye_tile = iota((LANES, LANES), 0) == iota((LANES, LANES), 1)
    first = pl.program_id(0) * groups
    for a in range(groups):
        at = pl.ds(a * LANES, LANES)
        total = total_ref[pl.ds(first + a, 1), :]
        scaling = lax.rsqrt(total / width_all + norm_eps)
        line = jnp.where(eye_tile, jnp.broadcast_to(scaling, (LANES, LANES)), 0.0)
        col = jnp.sum(line, axis=1, keepdims=True)
        h = hid_ref[at]
        out_ref[at] = h
        normed_ref[at] = (h.astype(F32) * col * gain_ref[...]).astype(BF16)


def local(
    gate_in, value_in, out_gate, residual, filters, kept_index, kept_owner, skip_bias, norm_gain
):
    tok, width = gate_in.shape
    slots, length = filters.shape[2:]
    seqo, seqi, chan = (lax.axis_size(n) for n in ("seqo", "seqi", "chan"))
    owners = seqo * seqi
    per = tok // LANES
    rows = per * owners
    pairs = slots // 2
    outer_tab, twist_tab, inner_tab = tables(rows)
    vmem = pl.BlockSpec(memory_space=pltpu.VMEM)
    hbm = pl.BlockSpec(memory_space=pl.ANY)
    pair_shape = (pairs, rows, 2 * LANES)
    dma = pltpu.SemaphoreType.DMA
    hidden, total = pl.pallas_call(
        functools.partial(main_kernel, slots, seqo, seqi, chan),
        out_shape=(
            jax.ShapeDtypeStruct((tok, width), BF16),
            jax.ShapeDtypeStruct((per, LANES), F32),
        ),
        in_specs=[vmem] * 3 + [hbm] * 8,
        out_specs=(hbm, vmem),
        scratch_shapes=[
            pltpu.VMEM((tok, width), BF16),
            pltpu.VMEM((tok, width), BF16),
            pltpu.VMEM((tok, width), BF16),
            pltpu.VMEM((tok, width), BF16),
            pltpu.VMEM((slots, length), BF16),
            pltpu.VMEM(outer_tab.shape, BF16),
            pltpu.VMEM(twist_tab.shape, F32),
            pltpu.VMEM(inner_tab.shape, BF16),
            pltpu.VMEM((tok, width), BF16),
            pltpu.VMEM((tok, width), F32),
            pltpu.VMEM((tok, width), BF16),
            pltpu.VMEM((slots, rows, LANES), F32),
            pltpu.VMEM((slots * rows, LANES), F32),
            pltpu.VMEM(pair_shape, BF16),
            pltpu.VMEM(pair_shape, BF16),
            pltpu.VMEM(pair_shape, BF16),
            pltpu.VMEM((slots, rows, 2 * LANES), F32),
            pltpu.VMEM((rows, 2 * LANES), BF16),
            pltpu.VMEM((rows, 2 * LANES), BF16),
            pltpu.VMEM(pair_shape, BF16),
            pltpu.VMEM(pair_shape, BF16),
            pltpu.VMEM((per, LANES), F32),
            pltpu.VMEM((chan, per, LANES), F32),
            dma((14,)),
            dma((1,)),
            dma((pairs,)),
            dma((pairs,)),
            dma((pairs,)),
            dma((pairs,)),
            dma((chan,)),
            dma((chan,)),
            dma((1,)),
        ],
        compiler_params=pltpu.CompilerParams(
            collective_id=0, has_side_effects=True, vmem_limit_bytes=60 * 1024 * 1024
        ),
        name="hyena",
    )(
        kept_index,
        kept_owner,
        skip_bias.reshape(1, width),
        gate_in,
        value_in,
        out_gate,
        residual,
        filters,
        outer_tab,
        twist_tab,
        inner_tab,
    )
    block = tok // 4
    rows_spec = pl.BlockSpec((block, width), lambda i: (i, 0))
    return pl.pallas_call(
        functools.partial(norm_kernel, width * chan),
        grid=(4,),
        out_shape=(jax.ShapeDtypeStruct((tok, width), BF16),) * 2,
        in_specs=[
            rows_spec,
            pl.BlockSpec((per, LANES), lambda i: (0, 0)),
            pl.BlockSpec((1, width), lambda i: (0, 0)),
        ],
        out_specs=(rows_spec, rows_spec),
        name="norm",
    )(hidden, total, norm_gain.reshape(1, width))


def solution(mesh):
    by_token = P(("seqo", "seqi"), "chan")
    in_specs = (
        by_token,
        by_token,
        by_token,
        by_token,
        P("chan", ("seqo", "seqi"), None, None),
        P("chan", None),
        P("chan", None),
        P("chan"),
        P("chan"),
    )
    return jax.shard_map(
        local, mesh=mesh, in_specs=in_specs, out_specs=(by_token, by_token), check_vma=False
    )
```

time: 190 us -> 49.5 us (0.26)
  the two profiles are of different devices: /device:TPU:0 before, /device:TPU:1 now
where the time goes in v1:
time: 49.5 us; the launch traced here: 49.3 us
  Pallas kernels  48.7 us (98%)
  between operations  0.64 us (1%)
    pallas_call x1, Pallas kernels, local(): pl.pallas_call(functools.partial(main_kernel, slots, seqo, seqi, chan), o...  44.4 us
    pallas_call x1, Pallas kernels, local(): pl.pallas_call(functools.partial(norm_kernel, width * chan), grid=(4,), o...  4.3 us

profile of v1, /device:TPU:1, one launch (start us, length us, event | category | flops | bytes accessed | tf_op | source)
XLA Modules:
  0.0 49.3 jit_solution(6808944409463187268)
XLA Ops:
  0.6 44.4 %hyena.1 = (bf16[2048,512]{1,0:T(8,128)(2,1)}, f32[16,128]{1,0:T(8,128)}) custom-call(s32[1,128]{1,0:T(1,128)} %index_ref.1, s32[1,128]{1,0:T(1,128)} %owner_ref.1, f32[1,512]{1,0:T(1,128)} %bitcast.3, bf16[2048,512]{1,0:T(8,128)(2,1)} %gate_hbm.1, bf16[2048,512]{1,0:T(8,128)(2,1)} %value_hbm.1, bf16[2048,512]{1,0:T(8,128)(2,1)} %og_hbm.1, ...), custom_call_target="tpu_custom_call" | custom-call | tf_op jit(solution)/shard_map/hyena/pallas_call | solution.py:417
  45.0 4.3 %norm.1 = (bf16[2048,512]{1,0:T(8,128)(2,1)}, bf16[2048,512]{1,0:T(8,128)(2,1)}) custom-call(bf16[2048,512]{1,0:T(8,128)(2,1)} %get-tuple-element.4.hid_ref, f32[16,128]{1,0:T(8,128)} %get-tuple-element.5.total_ref, f32[1,512]{1,0:T(1,128)} %bitcast.2), custom_call_target="tpu_custom_call" | custom-call | tf_op jit(solution)/shard_map/norm/pallas_call | solution.py:478

commit v2 on v1

--- a/solution.py
+++ b/solution.py
@@ -72,9 +72,10 @@
     twist,
     inner,
     gated,
-    base,
     hid,
     wide,
+    wide_og,
+    wide_base,
     fwide,
     sent,
     arrived,
@@ -135,6 +136,26 @@
         o = lax.rem(me + i, owners)
         return o, {"seqo": o // seqi, "seqi": lax.rem(o, seqi)}
 
+    def partner(dy, dx, dc):
+        y = lax.rem(lax.axis_index("seqo") + dy, seqo)
+        i = lax.axis_index("seqi")
+        x = lax.rem(i // 2 + dx, seqi // 2) * 2 + lax.rem(i + dc, 2)
+        return y * seqi + x, {"seqo": y, "seqi": x}
+
+    def ring(step, size):
+        return min(step, size - step)
+
+    steps = sorted(
+        (
+            (dy, dx, dc)
+            for dy in range(seqo)
+            for dx in range(seqi // 2)
+            for dc in range(2)
+            if dy or dx or dc
+        ),
+        key=lambda s: -ring(s[0], seqo) - ring(s[1], seqi // 2),
+    )
+
     def column(i):
         return {"chan": lax.rem(mez + i, chan)}
 
@@ -169,21 +190,24 @@
     spread = jnp.where(chan_at == jnp.broadcast_to(idx_col, (kmax, width)), 1.0, 0.0)
     picker = dot(select.astype(BF16), spread.astype(BF16)).astype(BF16)
 
+    def pick(x):
+        return lax.dot_general(picker, x, (((1,), (1,)), ((), ())), preferred_element_type=F32)
+
+    def lay_out(ref, picked, c):
+        for q in range(crow // LANES):
+            a = c * (crow // LANES) + q
+            for r in range(slots):
+                ref[r, pl.ds(a, owners, stride=per), :] = picked[
+                    r * owners : (r + 1) * owners, q * LANES : (q + 1) * LANES
+                ]
+
     for c in range(chunks):
         for cp in gate_loads(c):
             cp.wait()
         at = pl.ds(c * crow, crow)
         prod = (gate[at].astype(F32) * value[at].astype(F32)).astype(BF16)
         gated[at] = prod
-        picked = lax.dot_general(
-            picker, prod, (((1,), (1,)), ((), ())), preferred_element_type=F32
-        )
-        for q in range(crow // LANES):
-            a = c * (crow // LANES) + q
-            for r in range(slots):
-                wide[r, pl.ds(a, owners, stride=per), :] = picked[
-                    r * owners : (r + 1) * owners, q * LANES : (q + 1) * LANES
-                ]
+        lay_out(wide, pick(prod), c)
 
     def span(o):
         return pl.ds(pl.multiple_of(o * per, per), per)
@@ -194,8 +218,8 @@
         )
         mine.start()
 
-        def one(i, carry):
-            o, dev = plane(i)
+        for step in steps:
+            o, dev = partner(*step)
             pltpu.make_async_remote_copy(
                 src_ref=src.at[p, span(o)],
                 dst_ref=dst.at[p, span(me)],
@@ -204,9 +228,6 @@
                 device_id=dev,
                 device_id_type=MESH,
             ).start()
-            return carry
-
-        lax.fori_loop(1, owners, one, 0)
         mine.wait()
 
     def whole(p, src, dst, ssem, rsem):
@@ -310,32 +331,23 @@
     og_load.wait()
     res_load.wait()
     skip = skip_ref[...]
-
-    def base_step(a, carry):
+    picker_wide = picker.astype(F32)
+    other = jnp.where(jnp.sum(picker_wide, axis=0, keepdims=True) > 0.0, 0.0, 1.0)
+    skip_slot = jnp.sum(picker_wide * skip, axis=1, keepdims=True)
+
+    for c in range(chunks):
+        at = pl.ds(c * crow, crow)
+        og_slot = pick(og[at])
+        lay_out(wide_og, og_slot, c)
+        base_slot = pick(res[at]) + og_slot * (skip_slot * pick(gated[at]))
+        lay_out(wide_base, base_slot, c)
+
+    eye_tile = iota((LANES, LANES), 0) == iota((LANES, LANES), 1)
+
+    def rest_step(a, carry):
         at = pl.ds(pl.multiple_of(a * LANES, LANES), LANES)
-        base[at] = res[at].astype(F32) + og[at].astype(F32) * (skip * gated[at].astype(F32))
-        return carry
-
-    lax.fori_loop(0, per, base_step, 0)
-
-    for p in range(pairs):
-        whole(p, back, ret, bsend_sem, brecv_sem).wait_recv()
-        for ch in range(2):
-            wide[2 * p + ch] = ret[p, :, ch * LANES : (ch + 1) * LANES].astype(F32)
-
-    eye_tile = iota((LANES, LANES), 0) == iota((LANES, LANES), 1)
-
-    def final_step(a, carry):
-        at = pl.ds(pl.multiple_of(a * LANES, LANES), LANES)
-        got = jnp.concatenate(
-            [
-                wide[r, pl.ds(a, owners, stride=per), :]
-                for r in range(slots)
-            ],
-            axis=0,
-        ).astype(BF16)
-        conv = lax.dot_general(got, picker, (((0,), (0,)), ((), ())), preferred_element_type=F32)
-        out = (base[at] + og[at].astype(F32) * conv).astype(BF16)
+        out = res[at].astype(F32) + og[at].astype(F32) * (skip * gated[at].astype(F32))
+        out = (out * other).astype(BF16)
         hid[at] = out
         big = out.astype(F32)
         sq = big * big
@@ -347,9 +359,21 @@
         squares[pl.ds(a, 1), :] = jnp.sum(line, axis=0, keepdims=True)
         return carry
 
-    lax.fori_loop(0, per, final_step, 0)
-    hid_store = pltpu.make_async_copy(hid, hid_hbm, out_sem.at[0])
-    hid_store.start()
+    lax.fori_loop(0, per, rest_step, 0, unroll=2)
+
+    for p in range(pairs):
+        whole(p, back, ret, bsend_sem, brecv_sem).wait_recv()
+        for ch in range(2):
+            r = 2 * p + ch
+
+            def slot_step(o, acc):
+                at = pl.ds(pl.multiple_of(o * per, per), per)
+                conv = ret[p, at, ch * LANES : (ch + 1) * LANES].astype(F32)
+                h = (wide_base[r, at] + wide_og[r, at] * conv).astype(BF16).astype(F32)
+                wide[r, at] = h
+                return acc + h * h
+
+            squares[...] = lax.fori_loop(0, owners, slot_step, squares[...], unroll=8)
 
     def send_sums(i, carry):
         pltpu.make_async_remote_copy(
@@ -363,6 +387,20 @@
         return carry
 
     lax.fori_loop(1, chan, send_sums, 0)
+
+    def final_step(a, carry):
+        at = pl.ds(pl.multiple_of(a * LANES, LANES), LANES)
+        got = jnp.concatenate(
+            [wide[r, pl.ds(a, owners, stride=per), :] for r in range(slots)],
+            axis=0,
+        ).astype(BF16)
+        kept = lax.dot_general(got, picker, (((0,), (0,)), ((), ())), preferred_element_type=F32)
+        hid[at] = (hid[at].astype(F32) + kept).astype(BF16)
+        return carry
+
+    lax.fori_loop(0, per, final_step, 0, unroll=4)
+    hid_store = pltpu.make_async_copy(hid, hid_hbm, out_sem.at[0])
+    hid_store.start()
 
     def take_sums(i, acc):
         cp = pltpu.make_async_remote_copy(
@@ -432,8 +470,9 @@
             pltpu.VMEM(twist_tab.shape, F32),
             pltpu.VMEM(inner_tab.shape, BF16),
             pltpu.VMEM((tok, width), BF16),
-            pltpu.VMEM((tok, width), F32),
             pltpu.VMEM((tok, width), BF16),
+            pltpu.VMEM((slots, rows, LANES), F32),
+            pltpu.VMEM((slots, rows, LANES), F32),
             pltpu.VMEM((slots, rows, LANES), F32),
             pltpu.VMEM((slots * rows, LANES), F32),
             pltpu.VMEM(pair_shape, BF16),

time: 49.5 us -> 42.4 us (0.86)
  Pallas kernels: 48.7 us -> 41.6 us
    pallas_call x1, Pallas kernels: 44.4 us -> 37.3 us  [local(): pl.pallas_call(functools.partial(main_kernel, slots, seqo, seqi, chan), o...]
where the time goes in v2:
time: 42.4 us; the launch traced here: 42.2 us
  Pallas kernels  41.6 us (98%)
  between operations  0.64 us (2%)
    pallas_call x1, Pallas kernels, local(): pl.pallas_call(functools.partial(main_kernel, slots, seqo, seqi, chan), o...  37.3 us
    pallas_call x1, Pallas kernels, local(): pl.pallas_call(functools.partial(norm_kernel, width * chan), grid=(4,), o...  4.3 us

profile of v2, /device:TPU:1, one launch (start us, length us, event | category | flops | bytes accessed | tf_op | source)
XLA Modules:
  0.0 42.2 jit_solution(1213257268586971676)
XLA Ops:
  0.6 37.3 %hyena.1 = (bf16[2048,512]{1,0:T(8,128)(2,1)}, f32[16,128]{1,0:T(8,128)}) custom-call(s32[1,128]{1,0:T(1,128)} %index_ref.1, s32[1,128]{1,0:T(1,128)} %owner_ref.1, f32[1,512]{1,0:T(1,128)} %bitcast.3, bf16[2048,512]{1,0:T(8,128)(2,1)} %gate_hbm.1, bf16[2048,512]{1,0:T(8,128)(2,1)} %value_hbm.1, bf16[2048,512]{1,0:T(8,128)(2,1)} %og_hbm.1, ...), custom_call_target="tpu_custom_call" | custom-call | tf_op jit(solution)/shard_map/hyena/pallas_call | solution.py:455
  37.9 4.3 %norm.1 = (bf16[2048,512]{1,0:T(8,128)(2,1)}, bf16[2048,512]{1,0:T(8,128)(2,1)}) custom-call(bf16[2048,512]{1,0:T(8,128)(2,1)} %get-tuple-element.4.hid_ref, f32[16,128]{1,0:T(8,128)} %get-tuple-element.5.total_ref, f32[1,512]{1,0:T(1,128)} %bitcast.2), custom_call_target="tpu_custom_call" | custom-call | tf_op jit(solution)/shard_map/norm/pallas_call | solution.py:517

commit v3 on v2

--- a/solution.py
+++ b/solution.py
@@ -61,7 +61,7 @@
     outer_hbm,
     twist_hbm,
     inner_hbm,
-    hid_hbm,
+    hid,
     total_ref,
     gate,
     value,
@@ -72,10 +72,10 @@
     twist,
     inner,
     gated,
-    hid,
     wide,
     wide_og,
-    wide_base,
+    wide_res,
+    skip_slot,
     fwide,
     sent,
     arrived,
@@ -95,7 +95,6 @@
     brecv_sem,
     zsend_sem,
     zrecv_sem,
-    out_sem,
 ):
     owners = seqo * seqi
     pairs = slots // 2
@@ -287,7 +286,7 @@
                 spec[2 * p + ch, at] = got[ch] * scale
             return carry
 
-        return lax.fori_loop(0, rows // tile, step, carry)
+        return lax.fori_loop(0, rows // tile, step, carry, unroll=2)
 
     lax.fori_loop(0, pairs, filter_pair, 0)
 
@@ -311,7 +310,7 @@
                 turn_im[at, cut] = (ui * tc + ur * ts).astype(BF16)
             return carry
 
-        lax.fori_loop(0, rows // tile, step, 0)
+        lax.fori_loop(0, rows // tile, step, 0, unroll=2)
 
         def step_back(k, carry):
             at = pl.ds(pl.multiple_of(k * tile, tile), tile)
@@ -322,7 +321,7 @@
             back[p, at] = y.astype(BF16)
             return carry
 
-        lax.fori_loop(0, rows // tile, step_back, 0)
+        lax.fori_loop(0, rows // tile, step_back, 0, unroll=2)
         exchange(p, back, ret, bsend_sem, brecv_sem)
         return carry
 
@@ -333,14 +332,14 @@
     skip = skip_ref[...]
     picker_wide = picker.astype(F32)
     other = jnp.where(jnp.sum(picker_wide, axis=0, keepdims=True) > 0.0, 0.0, 1.0)
-    skip_slot = jnp.sum(picker_wide * skip, axis=1, keepdims=True)
+    skip_slot[...] = jnp.broadcast_to(
+        jnp.sum(picker_wide * skip, axis=1, keepdims=True), skip_slot.shape
+    )
 
     for c in range(chunks):
         at = pl.ds(c * crow, crow)
-        og_slot = pick(og[at])
-        lay_out(wide_og, og_slot, c)
-        base_slot = pick(res[at]) + og_slot * (skip_slot * pick(gated[at]))
-        lay_out(wide_base, base_slot, c)
+        lay_out(wide_og, pick(og[at]), c)
+        lay_out(wide_res, pick(res[at]), c)
 
     eye_tile = iota((LANES, LANES), 0) == iota((LANES, LANES), 1)
 
@@ -349,13 +348,8 @@
         out = res[at].astype(F32) + og[at].astype(F32) * (skip * gated[at].astype(F32))
         out = (out * other).astype(BF16)
         hid[at] = out
-        big = out.astype(F32)
-        sq = big * big
-        part = sq[:, :LANES]
-        for j in range(1, width // LANES):
-            part = part + sq[:, j * LANES : (j + 1) * LANES]
-        row_sum = jnp.sum(part, axis=1, keepdims=True)
-        line = jnp.where(eye_tile, jnp.broadcast_to(row_sum, (LANES, LANES)), 0.0)
+        gram = lax.dot_general(out, out, (((1,), (1,)), ((), ())), preferred_element_type=F32)
+        line = jnp.where(eye_tile, gram, 0.0)
         squares[pl.ds(a, 1), :] = jnp.sum(line, axis=0, keepdims=True)
         return carry
 
@@ -369,7 +363,8 @@
             def slot_step(o, acc):
                 at = pl.ds(pl.multiple_of(o * per, per), per)
                 conv = ret[p, at, ch * LANES : (ch + 1) * LANES].astype(F32)
-                h = (wide_base[r, at] + wide_og[r, at] * conv).astype(BF16).astype(F32)
+                bias = skip_slot[pl.ds(r * owners + o, 1), :] * wide[r, at]
+                h = (wide_res[r, at] + wide_og[r, at] * (conv + bias)).astype(BF16).astype(F32)
                 wide[r, at] = h
                 return acc + h * h
 
@@ -399,8 +394,6 @@
         return carry
 
     lax.fori_loop(0, per, final_step, 0, unroll=4)
-    hid_store = pltpu.make_async_copy(hid, hid_hbm, out_sem.at[0])
-    hid_store.start()
 
     def take_sums(i, acc):
         cp = pltpu.make_async_remote_copy(
@@ -419,22 +412,30 @@
     for p in range(pairs):
         whole(p, sent, arrived, send_sem, recv_sem).wait_send()
         whole(p, back, ret, bsend_sem, brecv_sem).wait_send()
-    hid_store.wait()
-
-
-def norm_kernel(width_all, hid_ref, total_ref, gain_ref, out_ref, normed_ref):
-    groups = hid_ref.shape[0] // LANES
+
+
+def norm_kernel(width_all, hid, total_ref, gain_ref, out_hbm, normed_hbm, normed, sem):
+    keep = pltpu.make_async_copy(hid, out_hbm, sem.at[0])
+    keep.start()
+    tok = hid.shape[0]
     eye_tile = iota((LANES, LANES), 0) == iota((LANES, LANES), 1)
-    first = pl.program_id(0) * groups
-    for a in range(groups):
-        at = pl.ds(a * LANES, LANES)
-        total = total_ref[pl.ds(first + a, 1), :]
-        scaling = lax.rsqrt(total / width_all + norm_eps)
-        line = jnp.where(eye_tile, jnp.broadcast_to(scaling, (LANES, LANES)), 0.0)
-        col = jnp.sum(line, axis=1, keepdims=True)
-        h = hid_ref[at]
-        out_ref[at] = h
-        normed_ref[at] = (h.astype(F32) * col * gain_ref[...]).astype(BF16)
+    block = 2 * LANES
+
+    def store(b):
+        at = pl.ds(b * block, block)
+        return pltpu.make_async_copy(normed.at[at], normed_hbm.at[at], sem.at[b + 1])
+
+    for b in range(tok // block):
+        for a in range(b * block // LANES, (b + 1) * block // LANES):
+            at = pl.ds(a * LANES, LANES)
+            scaling = lax.rsqrt(total_ref[pl.ds(a, 1), :] / width_all + norm_eps)
+            line = jnp.where(eye_tile, jnp.broadcast_to(scaling, (LANES, LANES)), 0.0)
+            col = jnp.sum(line, axis=1, keepdims=True)
+            normed[at] = (hid[at].astype(F32) * col * gain_ref[...]).astype(BF16)
+        store(b).start()
+    for b in range(tok // block):
+        store(b).wait()
+    keep.wait()
 
 
 def local(
@@ -455,11 +456,11 @@
     hidden, total = pl.pallas_call(
         functools.partial(main_kernel, slots, seqo, seqi, chan),
         out_shape=(
-            jax.ShapeDtypeStruct((tok, width), BF16),
-            jax.ShapeDtypeStruct((per, LANES), F32),
+            pltpu.VMEM((tok, width), BF16),
+            pltpu.VMEM((per, LANES), F32),
         ),
         in_specs=[vmem] * 3 + [hbm] * 8,
-        out_specs=(hbm, vmem),
+        out_specs=(vmem, vmem),
         scratch_shapes=[
             pltpu.VMEM((tok, width), BF16),
             pltpu.VMEM((tok, width), BF16),
@@ -470,10 +471,10 @@
             pltpu.VMEM(twist_tab.shape, F32),
             pltpu.VMEM(inner_tab.shape, BF16),
             pltpu.VMEM((tok, width), BF16),
-            pltpu.VMEM((tok, width), BF16),
             pltpu.VMEM((slots, rows, LANES), F32),
             pltpu.VMEM((slots, rows, LANES), F32),
             pltpu.VMEM((slots, rows, LANES), F32),
+            pltpu.VMEM((slots * owners, LANES), F32),
             pltpu.VMEM((slots * rows, LANES), F32),
             pltpu.VMEM(pair_shape, BF16),
             pltpu.VMEM(pair_shape, BF16),
@@ -493,7 +494,6 @@
             dma((pairs,)),
             dma((chan,)),
             dma((chan,)),
-            dma((1,)),
         ],
         compiler_params=pltpu.CompilerParams(
             collective_id=0, has_side_effects=True, vmem_limit_bytes=60 * 1024 * 1024
@@ -512,20 +512,19 @@
         twist_tab,
         inner_tab,
     )
-    block = tok // 4
-    rows_spec = pl.BlockSpec((block, width), lambda i: (i, 0))
     return pl.pallas_call(
         functools.partial(norm_kernel, width * chan),
-        grid=(4,),
         out_shape=(jax.ShapeDtypeStruct((tok, width), BF16),) * 2,
-        in_specs=[
-            rows_spec,
-            pl.BlockSpec((per, LANES), lambda i: (0, 0)),
-            pl.BlockSpec((1, width), lambda i: (0, 0)),
-        ],
-        out_specs=(rows_spec, rows_spec),
+        in_specs=[vmem] * 3,
+        out_specs=(hbm, hbm),
+        scratch_shapes=[pltpu.VMEM((tok, width), BF16), dma((tok // (2 * LANES) + 1,))],
+        compiler_params=pltpu.CompilerParams(vmem_limit_bytes=8 * 1024 * 1024),
         name="norm",
-    )(hidden, total, norm_gain.reshape(1, width))
+    )(
+        pltpu.with_memory_space_constraint(hidden, pltpu.VMEM),
+        pltpu.with_memory_space_constraint(total, pltpu.VMEM),
+        norm_gain.reshape(1, width),
+    )
 
 
 def solution(mesh):

time: 42.4 us -> 39.2 us (0.925)
  Pallas kernels: 41.6 us -> 38.4 us
    pallas_call x1, Pallas kernels: 4.3 us -> 2.08 us  [local(): pl.pallas_call(functools.partial(norm_kernel, width * chan), out_shape=(j...]
    pallas_call x1, Pallas kernels: 37.3 us -> 36.3 us  [local(): pl.pallas_call(functools.partial(main_kernel, slots, seqo, seqi, chan), o...]
where the time goes in v3:
time: 39.2 us; the launch traced here: 39.1 us
  Pallas kernels  38.4 us (98%)
  between operations  0.66 us (2%)
    pallas_call x1, Pallas kernels, local(): pl.pallas_call(functools.partial(main_kernel, slots, seqo, seqi, chan), o...  36.3 us
    pallas_call x1, Pallas kernels, local(): pl.pallas_call(functools.partial(norm_kernel, width * chan), out_shape=(j...  2.08 us

profile of v3, /device:TPU:1, one launch (start us, length us, event | category | flops | bytes accessed | tf_op | source)
XLA Modules:
  0.0 39.1 jit_solution(4085068224167295371)
XLA Ops:
  0.6 0.0 copy-start
  0.6 36.3 %hyena.1 = (bf16[2048,512]{1,0:T(8,128)(2,1)S(1)}, f32[16,128]{1,0:T(8,128)S(1)}) custom-call(s32[1,128]{1,0:T(1,128)} %index_ref.1, s32[1,128]{1,0:T(1,128)} %owner_ref.1, f32[1,512]{1,0:T(1,128)} %bitcast.3, bf16[2048,512]{1,0:T(8,128)(2,1)} %gate_hbm.1, bf16[2048,512]{1,0:T(8,128)(2,1)} %value_hbm.1, bf16[2048,512]{1,0:T(8,128)(2,1)} %og_hbm.1, ...), custom_call_target="tpu_custom_call" | custom-call | tf_op jit(solution)/shard_map/hyena/pallas_call | solution.py:456
  37.0 0.0 copy-done
  37.0 2.1 %norm.1 = (bf16[2048,512]{1,0:T(8,128)(2,1)}, bf16[2048,512]{1,0:T(8,128)(2,1)}) custom-call(bf16[2048,512]{1,0:T(8,128)(2,1)S(1)} %get-tuple-element.4.hid, f32[16,128]{1,0:T(8,128)S(1)} %get-tuple-element.5.total_ref, f32[1,512]{1,0:T(1,128)S(1)} %bitcast.2), custom_call_target="tpu_custom_call" | custom-call | tf_op jit(solution)/shard_map/norm/pallas_call | solution.py:515
Async XLA Ops:
  0.6 36.3 %copy-start = (f32[512]{0:T(512)S(1)}, f32[512]{0:T(512)}, u32[]{:S(2)}) copy-start(f32[512]{0:T(512)} %param.20) | copy-start | bytes 6148

commit v4 on v3

--- a/solution.py
+++ b/solution.py
@@ -28,13 +28,17 @@
     inner_at = np.arange(LANES, dtype=np.float64)
     twist = 2.0 * np.pi * np.outer(step, inner_at - LANES / 2) / (2 * rows * LANES)
     inner = 2.0 * np.pi * np.outer(inner_at, inner_at) / LANES
-    outer_tab = np.stack([*split_table(np.cos(outer)), *split_table(-np.sin(outer))])
-    twist_tab = np.stack([np.cos(twist), np.sin(twist)]).astype(np.float32)
+    order = np.concatenate([np.arange(rows // 2), np.arange(rows - 1, rows // 2 - 1, -1)])
+    cosine = np.cos(outer)[order]
+    halves = [cosine[:, 0::2], cosine[:, 1::2]]
+    outer_tab = np.stack([part for half in halves for part in split_table(half)])
+    outer_back = np.stack([part for half in halves for part in split_table(half.T)])
+    twist_tab = np.stack([np.cos(twist)[order], np.sin(twist)[order]]).astype(np.float32)
     cos, sin = np.cos(inner), np.sin(inner)
     forward = np.block([[cos, -sin], [sin, cos]])
     back = np.block([[cos, sin], [-sin, cos]])
     inner_tab = np.stack([*split_table(forward), *split_table(back)])
-    return outer_tab, twist_tab, inner_tab
+    return outer_tab, outer_back, twist_tab, inner_tab
 
 
 def dot(a, b):
@@ -59,6 +63,7 @@
     res_hbm,
     filt_hbm,
     outer_hbm,
+    outback_hbm,
     twist_hbm,
     inner_hbm,
     hid,
@@ -69,6 +74,7 @@
     res,
     filt,
     outer,
+    outback,
     twist,
     inner,
     gated,
@@ -81,8 +87,6 @@
     arrived,
     fpair,
     spec,
-    turn_re,
-    turn_im,
     back,
     ret,
     squares,
@@ -106,7 +110,6 @@
     mez = lax.axis_index("chan")
     chunks = 4
     crow = tok // chunks
-    tile = 256
 
     def load(src, dst, k):
         return pltpu.make_async_copy(src, dst, load_sem.at[k])
@@ -128,7 +131,8 @@
     inner_load = load(inner_hbm, inner, nl + 3)
     og_load = load(og_hbm, og, nl + 4)
     res_load = load(res_hbm, res, nl + 5)
-    for cp in (filt_load, outer_load, twist_load, inner_load, og_load, res_load):
+    outback_load = load(outback_hbm, outback, nl + 6)
+    for cp in (filt_load, outer_load, twist_load, inner_load, outback_load, og_load, res_load):
         cp.start()
 
     def plane(i):
@@ -189,12 +193,15 @@
     spread = jnp.where(chan_at == jnp.broadcast_to(idx_col, (kmax, width)), 1.0, 0.0)
     picker = dot(select.astype(BF16), spread.astype(BF16)).astype(BF16)
 
+    def place(a):
+        return a % 2 * (per // 2) + a // 2
+
     def pick(x):
         return lax.dot_general(picker, x, (((1,), (1,)), ((), ())), preferred_element_type=F32)
 
     def lay_out(ref, picked, c):
         for q in range(crow // LANES):
-            a = c * (crow // LANES) + q
+            a = place(c * (crow // LANES) + q)
             for r in range(slots):
                 ref[r, pl.ds(a, owners, stride=per), :] = picked[
                     r * owners : (r + 1) * owners, q * LANES : (q + 1) * LANES
@@ -249,12 +256,16 @@
 
     filt_load.wait()
 
-    def unfold(a, carry):
-        taps = filt[:, pl.ds(pl.multiple_of(a * LANES, LANES), LANES)].astype(F32)
-        fwide[pl.ds(a, slots, stride=rows), :] = taps
-        return carry
-
-    lax.fori_loop(0, rows, unfold, 0, unroll=8)
+    half = rows // 2
+
+    def unfold(m, carry):
+        taps = filt[:, pl.ds(pl.multiple_of(m * 8 * LANES, 8 * LANES), 8 * LANES)].astype(F32)
+        for i in range(8):
+            at = pl.ds(i % 2 * half + i // 2 + 4 * m, slots, stride=rows)
+            fwide[at, :] = taps[:, i * LANES : (i + 1) * LANES]
+        return carry
+
+    lax.fori_loop(0, rows // 8, unfold, 0, unroll=2)
     for r in range(slots):
         fpair[r // 2, :, (r % 2) * LANES : (r % 2 + 1) * LANES] = fwide[
             r * rows : (r + 1) * rows, :
@@ -263,10 +274,21 @@
     outer_load.wait()
     twist_load.wait()
     inner_load.wait()
-
-    def forward(x, at):
-        re = dot(outer[0, at], x) + dot(outer[1, at], x)
-        im = dot(outer[2, at], x) + dot(outer[3, at], x)
+    outback_load.wait()
+
+    def parity(x):
+        groups = x.astype(F32).reshape(owners, 2, per // 2, 2 * LANES)
+        return tuple(groups[:, i].reshape(half, 2 * LANES).astype(BF16) for i in range(2))
+
+    def forward(even, odd):
+        low, high = pl.ds(0, half), pl.ds(half, half)
+        p = [dot(outer[0, at], even) + dot(outer[1, at], even) for at in (low, high)]
+        q = [dot(outer[2, at], odd) + dot(outer[3, at], odd) for at in (low, high)]
+        return [
+            twisted(at, p[i] + q[i], q[1 - i] - p[1 - i]) for i, at in enumerate((low, high))
+        ]
+
+    def twisted(at, re, im):
         tc, ts = twist[0, at], twist[1, at]
         out = []
         for ch in range(2):
@@ -279,49 +301,43 @@
     scale = 1.0 / (rows * LANES)
 
     def filter_pair(p, carry):
-        def step(k, carry):
-            at = pl.ds(pl.multiple_of(k * tile, tile), tile)
-            got = forward(fpair[p], at)
+        got = forward(fpair[p, pl.ds(0, half)], fpair[p, pl.ds(half, half)])
+        for i in range(2):
             for ch in range(2):
-                spec[2 * p + ch, at] = got[ch] * scale
-            return carry
-
-        return lax.fori_loop(0, rows // tile, step, carry, unroll=2)
+                spec[2 * p + ch, pl.ds(i * half, half)] = got[i][ch] * scale
+        return carry
 
     lax.fori_loop(0, pairs, filter_pair, 0)
 
     def convolve_pair(p, carry):
         whole(p, sent, arrived, send_sem, recv_sem).wait_recv()
-
-        def step(k, carry):
-            at = pl.ds(pl.multiple_of(k * tile, tile), tile)
-            got = forward(arrived[p], at)
+        got = forward(*parity(arrived[p]))
+        turns = []
+        for i in range(2):
+            at = pl.ds(i * half, half)
             tc, ts = twist[0, at], twist[1, at]
+            us, vs = [], []
             for ch in range(2):
-                cut = slice(ch * LANES, (ch + 1) * LANES)
                 kern = spec[2 * p + ch, at]
-                sr, si = got[ch][:, :LANES], got[ch][:, LANES:]
+                sr, si = got[i][ch][:, :LANES], got[i][ch][:, LANES:]
                 kr, ki = kern[:, :LANES], kern[:, LANES:]
                 joint = jnp.concatenate([sr * kr - si * ki, sr * ki + si * kr], axis=1)
                 joint = joint.astype(BF16)
                 u = dot(joint, inner[2]) + dot(joint, inner[3])
                 ur, ui = u[:, :LANES], u[:, LANES:]
-                turn_re[at, cut] = (ur * tc - ui * ts).astype(BF16)
-                turn_im[at, cut] = (ui * tc + ur * ts).astype(BF16)
-            return carry
-
-        lax.fori_loop(0, rows // tile, step, 0, unroll=2)
-
-        def step_back(k, carry):
-            at = pl.ds(pl.multiple_of(k * tile, tile), tile)
-            u, v = turn_re[...], turn_im[...]
-            y = (dot(outer[0, at], u) + dot(outer[1, at], u)) + (
-                dot(outer[2, at], v) + dot(outer[3, at], v)
-            )
-            back[p, at] = y.astype(BF16)
-            return carry
-
-        lax.fori_loop(0, rows // tile, step_back, 0, unroll=2)
+                us.append(ur * tc - ui * ts)
+                vs.append(ui * tc + ur * ts)
+            turns.append((jnp.concatenate(us, axis=1), jnp.concatenate(vs, axis=1)))
+        halves = []
+        for parity_at, sign in ((0, -1.0), (1, 1.0)):
+            y = None
+            for i in range(2):
+                at = slice(i * half, (i + 1) * half)
+                w = (turns[i][0] + sign * turns[1 - i][1]).astype(BF16)
+                term = dot(outback[2 * parity_at, :, at], w) + dot(outback[2 * parity_at + 1, :, at], w)
+                y = term if y is None else y + term
+            halves.append(y.reshape(owners, 1, per // 2, 2 * LANES))
+        back[p] = jnp.concatenate(halves, axis=1).reshape(rows, 2 * LANES).astype(BF16)
         exchange(p, back, ret, bsend_sem, brecv_sem)
         return carry
 
@@ -350,7 +366,7 @@
         hid[at] = out
         gram = lax.dot_general(out, out, (((1,), (1,)), ((), ())), preferred_element_type=F32)
         line = jnp.where(eye_tile, gram, 0.0)
-        squares[pl.ds(a, 1), :] = jnp.sum(line, axis=0, keepdims=True)
+        squares[pl.ds(place(a), 1), :] = jnp.sum(line, axis=0, keepdims=True)
         return carry
 
     lax.fori_loop(0, per, rest_step, 0, unroll=2)
@@ -386,7 +402,7 @@
     def final_step(a, carry):
         at = pl.ds(pl.multiple_of(a * LANES, LANES), LANES)
         got = jnp.concatenate(
-            [wide[r, pl.ds(a, owners, stride=per), :] for r in range(slots)],
+            [wide[r, pl.ds(place(a), owners, stride=per), :] for r in range(slots)],
             axis=0,
         ).astype(BF16)
         kept = lax.dot_general(got, picker, (((0,), (0,)), ((), ())), preferred_element_type=F32)
@@ -428,7 +444,8 @@
     for b in range(tok // block):
         for a in range(b * block // LANES, (b + 1) * block // LANES):
             at = pl.ds(a * LANES, LANES)
-            scaling = lax.rsqrt(total_ref[pl.ds(a, 1), :] / width_all + norm_eps)
+            row = a % 2 * (tok // LANES // 2) + a // 2
+            scaling = lax.rsqrt(total_ref[pl.ds(row, 1), :] / width_all + norm_eps)
             line = jnp.where(eye_tile, jnp.broadcast_to(scaling, (LANES, LANES)), 0.0)
             col = jnp.sum(line, axis=1, keepdims=True)
             normed[at] = (hid[at].astype(F32) * col * gain_ref[...]).astype(BF16)
@@ -448,7 +465,7 @@
     per = tok // LANES
     rows = per * owners
     pairs = slots // 2
-    outer_tab, twist_tab, inner_tab = tables(rows)
+    outer_tab, outer_back, twist_tab, inner_tab = tables(rows)
     vmem = pl.BlockSpec(memory_space=pltpu.VMEM)
     hbm = pl.BlockSpec(memory_space=pl.ANY)
     pair_shape = (pairs, rows, 2 * LANES)
@@ -459,7 +476,7 @@
             pltpu.VMEM((tok, width), BF16),
             pltpu.VMEM((per, LANES), F32),
         ),
-        in_specs=[vmem] * 3 + [hbm] * 8,
+        in_specs=[vmem] * 3 + [hbm] * 9,
         out_specs=(vmem, vmem),
         scratch_shapes=[
             pltpu.VMEM((tok, width), BF16),
@@ -468,6 +485,7 @@
             pltpu.VMEM((tok, width), BF16),
             pltpu.VMEM((slots, length), BF16),
             pltpu.VMEM(outer_tab.shape, BF16),
+            pltpu.VMEM(outer_back.shape, BF16),
             pltpu.VMEM(twist_tab.shape, F32),
             pltpu.VMEM(inner_tab.shape, BF16),
             pltpu.VMEM((tok, width), BF16),
@@ -475,18 +493,16 @@
             pltpu.VMEM((slots, rows, LANES), F32),
             pltpu.VMEM((slots, rows, LANES), F32),
             pltpu.VMEM((slots * owners, LANES), F32),
-            pltpu.VMEM((slots * rows, LANES), F32),
+            pltpu.VMEM((8 * rows, LANES), F32),
             pltpu.VMEM(pair_shape, BF16),
             pltpu.VMEM(pair_shape, BF16),
             pltpu.VMEM(pair_shape, BF16),
             pltpu.VMEM((slots, rows, 2 * LANES), F32),
-            pltpu.VMEM((rows, 2 * LANES), BF16),
-            pltpu.VMEM((rows, 2 * LANES), BF16),
             pltpu.VMEM(pair_shape, BF16),
             pltpu.VMEM(pair_shape, BF16),
             pltpu.VMEM((per, LANES), F32),
             pltpu.VMEM((chan, per, LANES), F32),
-            dma((14,)),
+            dma((15,)),
             dma((1,)),
             dma((pairs,)),
             dma((pairs,)),
@@ -509,6 +525,7 @@
         residual,
         filters,
         outer_tab,
+        outer_back,
         twist_tab,
         inner_tab,
     )

time: 39.2 us -> 38.6 us (0.985)
  Pallas kernels: 38.4 us -> 37.9 us
    pallas_call x1, Pallas kernels: 36.3 us -> 35.8 us  [local(): pl.pallas_call(functools.partial(main_kernel, slots, seqo, seqi, chan), o...]
where the time goes in v4:
time: 38.6 us; the launch traced here: 38.5 us
  Pallas kernels  37.9 us (98%)
  between operations  0.66 us (2%)
    pallas_call x1, Pallas kernels, local(): pl.pallas_call(functools.partial(main_kernel, slots, seqo, seqi, chan), o...  35.8 us
    pallas_call x1, Pallas kernels, local(): pl.pallas_call(functools.partial(norm_kernel, width * chan), out_shape=(j...  2.08 us

profile of v4, /device:TPU:1, one launch (start us, length us, event | category | flops | bytes accessed | tf_op | source)
XLA Modules:
  0.0 38.5 jit_solution(13764103246689341664)
XLA Ops:
  0.6 0.0 copy-start
  0.6 35.8 %hyena.1 = (bf16[2048,512]{1,0:T(8,128)(2,1)S(1)}, f32[16,128]{1,0:T(8,128)S(1)}) custom-call(s32[1,128]{1,0:T(1,128)} %index_ref.1, s32[1,128]{1,0:T(1,128)} %owner_ref.1, f32[1,512]{1,0:T(1,128)} %bitcast.3, bf16[2048,512]{1,0:T(8,128)(2,1)} %gate_hbm.1, bf16[2048,512]{1,0:T(8,128)(2,1)} %value_hbm.1, bf16[2048,512]{1,0:T(8,128)(2,1)} %og_hbm.1, ...), custom_call_target="tpu_custom_call" | custom-call | tf_op jit(solution)/shard_map/hyena/pallas_call | solution.py:473
  36.4 0.0 copy-done
  36.5 2.1 %norm.1 = (bf16[2048,512]{1,0:T(8,128)(2,1)}, bf16[2048,512]{1,0:T(8,128)(2,1)}) custom-call(bf16[2048,512]{1,0:T(8,128)(2,1)S(1)} %get-tuple-element.4.hid, f32[16,128]{1,0:T(8,128)S(1)} %get-tuple-element.5.total_ref, f32[1,512]{1,0:T(1,128)S(1)} %bitcast.2), custom_call_target="tpu_custom_call" | custom-call | tf_op jit(solution)/shard_map/norm/pallas_call | solution.py:532
Async XLA Ops:
  0.6 35.8 %copy-start = (f32[512]{0:T(512)S(1)}, f32[512]{0:T(512)}, u32[]{:S(2)}) copy-start(f32[512]{0:T(512)} %param.21) | copy-start | bytes 6148

commit v5 on v4

--- a/solution.py
+++ b/solution.py
@@ -90,6 +90,7 @@
     back,
     ret,
     squares,
+    own_sums,
     parts,
     load_sem,
     local_sem,
@@ -164,16 +165,10 @@
 
     barrier = pltpu.get_barrier_semaphore()
 
-    def greet_plane(i, carry):
-        pl.semaphore_signal(barrier, inc=1, device_id=plane(i)[1], device_id_type=MESH)
-        return carry
-
-    def greet_column(i, carry):
+    for step in steps:
+        pl.semaphore_signal(barrier, inc=1, device_id=partner(*step)[1], device_id_type=MESH)
+    for i in range(1, chan):
         pl.semaphore_signal(barrier, inc=1, device_id=column(i), device_id_type=MESH)
-        return carry
-
-    lax.fori_loop(1, owners, greet_plane, 0)
-    lax.fori_loop(1, chan, greet_column, 0)
 
     kmax = index_ref.shape[1]
     own_row = jnp.broadcast_to(owner_ref[...].astype(F32), (kmax, kmax))
@@ -386,18 +381,19 @@
 
             squares[...] = lax.fori_loop(0, owners, slot_step, squares[...], unroll=8)
 
-    def send_sums(i, carry):
+    def send_sums(i):
         pltpu.make_async_remote_copy(
-            src_ref=squares,
+            src_ref=own_sums,
             dst_ref=parts.at[i],
             send_sem=zsend_sem.at[i],
             recv_sem=zrecv_sem.at[i],
             device_id=column(i),
             device_id_type=MESH,
         ).start()
-        return carry
-
-    lax.fori_loop(1, chan, send_sums, 0)
+
+    own_sums[...] = squares[...].astype(BF16)
+    for i in (4, 3, 5, 2, 6, 1, 7) if chan == 8 else range(1, chan):
+        send_sums(i)
 
     def final_step(a, carry):
         at = pl.ds(pl.multiple_of(a * LANES, LANES), LANES)
@@ -413,7 +409,7 @@
 
     def take_sums(i, acc):
         cp = pltpu.make_async_remote_copy(
-            src_ref=squares,
+            src_ref=own_sums,
             dst_ref=parts.at[i],
             send_sem=zsend_sem.at[i],
             recv_sem=zrecv_sem.at[i],
@@ -421,9 +417,9 @@
             device_id_type=MESH,
         )
         cp.wait()
-        return acc + parts[i]
-
-    total_ref[...] = lax.fori_loop(1, chan, take_sums, squares[...])
+        return acc + parts[i].astype(F32)
+
+    total_ref[...] = lax.fori_loop(1, chan, take_sums, own_sums[...].astype(F32))
 
     for p in range(pairs):
         whole(p, sent, arrived, send_sem, recv_sem).wait_send()
@@ -435,7 +431,7 @@
     keep.start()
     tok = hid.shape[0]
     eye_tile = iota((LANES, LANES), 0) == iota((LANES, LANES), 1)
-    block = 2 * LANES
+    block = 4 * LANES
 
     def store(b):
         at = pl.ds(b * block, block)
@@ -501,7 +497,8 @@
             pltpu.VMEM(pair_shape, BF16),
             pltpu.VMEM(pair_shape, BF16),
             pltpu.VMEM((per, LANES), F32),
-            pltpu.VMEM((chan, per, LANES), F32),
+            pltpu.VMEM((per, LANES), BF16),
+            pltpu.VMEM((chan, per, LANES), BF16),
             dma((15,)),
             dma((1,)),
             dma((pairs,)),
@@ -534,7 +531,7 @@
         out_shape=(jax.ShapeDtypeStruct((tok, width), BF16),) * 2,
         in_specs=[vmem] * 3,
         out_specs=(hbm, hbm),
-        scratch_shapes=[pltpu.VMEM((tok, width), BF16), dma((tok // (2 * LANES) + 1,))],
+        scratch_shapes=[pltpu.VMEM((tok, width), BF16), dma((tok // (4 * LANES) + 1,))],
         compiler_params=pltpu.CompilerParams(vmem_limit_bytes=8 * 1024 * 1024),
         name="norm",
     )(

time: 38.6 us -> 38.2 us (0.990)
  Pallas kernels: 37.9 us -> 37.5 us
where the time goes in v5:
time: 38.2 us; the launch traced here: 38.1 us
  Pallas kernels  37.5 us (98%)
  between operations  0.66 us (2%)
    pallas_call x1, Pallas kernels, local(): pl.pallas_call(functools.partial(main_kernel, slots, seqo, seqi, chan), o...  35.4 us
    pallas_call x1, Pallas kernels, local(): pl.pallas_call(functools.partial(norm_kernel, width * chan), out_shape=(j...  2.05 us

profile of v5, /device:TPU:1, one launch (start us, length us, event | category | flops | bytes accessed | tf_op | source)
XLA Modules:
  0.0 38.1 jit_solution(26595174931261195)
XLA Ops:
  0.6 0.0 copy-start
  0.6 35.4 %hyena.1 = (bf16[2048,512]{1,0:T(8,128)(2,1)S(1)}, f32[16,128]{1,0:T(8,128)S(1)}) custom-call(s32[1,128]{1,0:T(1,128)} %index_ref.1, s32[1,128]{1,0:T(1,128)} %owner_ref.1, f32[1,512]{1,0:T(1,128)} %bitcast.3, bf16[2048,512]{1,0:T(8,128)(2,1)} %gate_hbm.1, bf16[2048,512]{1,0:T(8,128)(2,1)} %value_hbm.1, bf16[2048,512]{1,0:T(8,128)(2,1)} %og_hbm.1, ...), custom_call_target="tpu_custom_call" | custom-call | tf_op jit(solution)/shard_map/hyena/pallas_call | solution.py:469
  36.1 0.0 copy-done
  36.1 2.0 %norm.1 = (bf16[2048,512]{1,0:T(8,128)(2,1)}, bf16[2048,512]{1,0:T(8,128)(2,1)}) custom-call(bf16[2048,512]{1,0:T(8,128)(2,1)S(1)} %get-tuple-element.4.hid, f32[16,128]{1,0:T(8,128)S(1)} %get-tuple-element.5.total_ref, f32[1,512]{1,0:T(1,128)S(1)} %bitcast.2), custom_call_target="tpu_custom_call" | custom-call | tf_op jit(solution)/shard_map/norm/pallas_call | solution.py:529
Async XLA Ops:
  0.6 35.4 %copy-start = (f32[512]{0:T(512)S(1)}, f32[512]{0:T(512)}, u32[]{:S(2)}) copy-start(f32[512]{0:T(512)} %param.21) | copy-start | bytes 6148

commit v6 on v5

--- a/solution.py
+++ b/solution.py
@@ -112,6 +112,40 @@
     chunks = 4
     crow = tok // chunks
 
+    def plane(i):
+        o = lax.rem(me + i, owners)
+        return o, {"seqo": o // seqi, "seqi": lax.rem(o, seqi)}
+
+    def partner(dy, dx, dc):
+        y = lax.rem(lax.axis_index("seqo") + dy, seqo)
+        i = lax.axis_index("seqi")
+        x = lax.rem(i // 2 + dx, seqi // 2) * 2 + lax.rem(i + dc, 2)
+        return y * seqi + x, {"seqo": y, "seqi": x}
+
+    def ring(step, size):
+        return min(step, size - step)
+
+    steps = sorted(
+        (
+            (dy, dx, dc)
+            for dy in range(seqo)
+            for dx in range(seqi // 2)
+            for dc in range(2)
+            if dy or dx or dc
+        ),
+        key=lambda s: -ring(s[0], seqo) - ring(s[1], seqi // 2),
+    )
+
+    def column(i):
+        return {"chan": lax.rem(mez + i, chan)}
+
+    barrier = pltpu.get_barrier_semaphore()
+
+    greets = [(-ring(s[0], seqo) - ring(s[1], seqi // 2), partner, s) for s in steps]
+    greets += [(-ring(i, chan), lambda i: (i, column(i)), (i,)) for i in range(1, chan)]
+    for _, whom, step in sorted(greets, key=lambda g: g[0]):
+        pl.semaphore_signal(barrier, inc=1, device_id=whom(*step)[1], device_id_type=MESH)
+
     def load(src, dst, k):
         return pltpu.make_async_copy(src, dst, load_sem.at[k])
 
@@ -135,40 +169,6 @@
     outback_load = load(outback_hbm, outback, nl + 6)
     for cp in (filt_load, outer_load, twist_load, inner_load, outback_load, og_load, res_load):
         cp.start()
-
-    def plane(i):
-        o = lax.rem(me + i, owners)
-        return o, {"seqo": o // seqi, "seqi": lax.rem(o, seqi)}
-
-    def partner(dy, dx, dc):
-        y = lax.rem(lax.axis_index("seqo") + dy, seqo)
-        i = lax.axis_index("seqi")
-        x = lax.rem(i // 2 + dx, seqi // 2) * 2 + lax.rem(i + dc, 2)
-        return y * seqi + x, {"seqo": y, "seqi": x}
-
-    def ring(step, size):
-        return min(step, size - step)
-
-    steps = sorted(
-        (
-            (dy, dx, dc)
-            for dy in range(seqo)
-            for dx in range(seqi // 2)
-            for dc in range(2)
-            if dy or dx or dc
-        ),
-        key=lambda s: -ring(s[0], seqo) - ring(s[1], seqi // 2),
-    )
-
-    def column(i):
-        return {"chan": lax.rem(mez + i, chan)}
-
-    barrier = pltpu.get_barrier_semaphore()
-
-    for step in steps:
-        pl.semaphore_signal(barrier, inc=1, device_id=partner(*step)[1], device_id_type=MESH)
-    for i in range(1, chan):
-        pl.semaphore_signal(barrier, inc=1, device_id=column(i), device_id_type=MESH)
 
     kmax = index_ref.shape[1]
     own_row = jnp.broadcast_to(owner_ref[...].astype(F32), (kmax, kmax))

time: 38.2 us -> 38.3 us (level)
  no operation moved by 1% of the time
where the time goes in v6:
time: 38.3 us; the launch traced here: 38.2 us
  Pallas kernels  37.5 us (98%)
  between operations  0.66 us (2%)
    pallas_call x1, Pallas kernels, local(): pl.pallas_call(functools.partial(main_kernel, slots, seqo, seqi, chan), o...  35.4 us
    pallas_call x1, Pallas kernels, local(): pl.pallas_call(functools.partial(norm_kernel, width * chan), out_shape=(j...  2.05 us

profile of v6, /device:TPU:1, one launch (start us, length us, event | category | flops | bytes accessed | tf_op | source)
XLA Modules:
  0.0 38.2 jit_solution(7606316325043141606)
XLA Ops:
  0.6 0.0 copy-start
  0.6 35.4 %hyena.1 = (bf16[2048,512]{1,0:T(8,128)(2,1)S(1)}, f32[16,128]{1,0:T(8,128)S(1)}) custom-call(s32[1,128]{1,0:T(1,128)} %index_ref.1, s32[1,128]{1,0:T(1,128)} %owner_ref.1, f32[1,512]{1,0:T(1,128)} %bitcast.3, bf16[2048,512]{1,0:T(8,128)(2,1)} %gate_hbm.1, bf16[2048,512]{1,0:T(8,128)(2,1)} %value_hbm.1, bf16[2048,512]{1,0:T(8,128)(2,1)} %og_hbm.1, ...), custom_call_target="tpu_custom_call" | custom-call | tf_op jit(solution)/shard_map/hyena/pallas_call | solution.py:469
  36.1 0.0 copy-done
  36.1 2.0 %norm.1 = (bf16[2048,512]{1,0:T(8,128)(2,1)}, bf16[2048,512]{1,0:T(8,128)(2,1)}) custom-call(bf16[2048,512]{1,0:T(8,128)(2,1)S(1)} %get-tuple-element.4.hid, f32[16,128]{1,0:T(8,128)S(1)} %get-tuple-element.5.total_ref, f32[1,512]{1,0:T(1,128)S(1)} %bitcast.2), custom_call_target="tpu_custom_call" | custom-call | tf_op jit(solution)/shard_map/norm/pallas_call | solution.py:529
Async XLA Ops:
  0.6 35.5 %copy-start = (f32[512]{0:T(512)S(1)}, f32[512]{0:T(512)}, u32[]{:S(2)}) copy-start(f32[512]{0:T(512)} %param.21) | copy-start | bytes 6148
